TPU v7x, 32 devices: a whole 2x2x4 slice. The times are simulated.
32 devices in a mesh: gx: 4 (over x, core), gy: 8 (over z, y).
Axes of the slice: x: 2, y: 2, z: 4, core: 2. Of those that a mesh axis runs over, the one named last changes fastest.
Arguments:
- text_feats: bfloat16 [16384, 1152], P(('gx', 'gy')), may hold values from -0.75 to 0.75
- proj: float32 [1152, 1152], P(('gx', 'gy')), may hold values from -0.1875 to 0.1875
- first_moment: float32 [1152, 1152], P(('gx', 'gy')), may hold values from -12 to 12
- second_moment: float32 [1152, 1152], P(('gx', 'gy')), may hold values from 0.1 to 10
- owners: int32 [1024, 5], P(('gx', 'gy')), may hold values from 0 to 31, all different within a row; in each aligned block of 32 rows (0 to 31, 32 to 63, ...) at most 6 rows name the same one
- blocks: int32 [1024, 5], P(('gx', 'gy')), may hold values from 0 to 11
- positives: int32 [16384], P(('gx', 'gy')), may hold values from 0 to 3071
- bank: bfloat16 [98304, 1152], P(('gx', 'gy')), may hold values from -0.1875 to 0.1875
Outputs:
- text_grad: bfloat16 [16384, 1152], P(('gx', 'gy'))
- new_proj: float32 [1152, 1152], P(('gx', 'gy'))
- new_first: float32 [1152, 1152], P(('gx', 'gy'))
- new_second: float32 [1152, 1152], P(('gx', 'gy'))
Inputs may be any that keep to these rules, and one draw needn't show every extreme that they name: `owners`: each row names 5 different owner devices, counted in the order gx then gy. Among the text blocks of one device no owner is named more than 6 times, and in some devices' blocks an owner is named exactly 6 times. `positives`: each text row's positive lies in its own device's bank, counted from that device's first bank row.
All inputs are finite; a program needn't handle non-finite values.
Results may differ from a plain program's by a relative error of at most 0.0095.
Values may be sent and summed in bfloat16 or wider, within the bound.
No kernel may reach another device: no remote copies, remote signals or barrier semaphores. Data moves between devices by JAX's collectives and lax.ppermute only.
A program may use at most 128 MiB of HBM per device.

v0:
```python
import jax
import jax.numpy as jnp
from jax import lax
from jax.sharding import PartitionSpec as P

TB = 16
BROWS = 256
HARD = 5


logit_scale = 20.0
logit_bias = -3.0
norm_eps = 1e-06
beta_one = 0.9
beta_two = 0.999
learn_rate = 0.001
decay_rate = 0.1
adam_eps = 1e-08
adam_step = 100.0
group_slots = 16


def answer_visits(incoming, block_tags, bank):
    slot_count = incoming.shape[0]
    embed_width = bank.shape[1]
    bank_blocks = bank.reshape(bank.shape[0] // BROWS, BROWS, embed_width)
    block_ids = block_tags.astype(jnp.int32)
    live_slots = (block_ids >= 0).astype(jnp.float32)
    safe_ids = jnp.maximum(block_ids, 0)
    groups = slot_count // group_slots

    def per_group(pieces):
        group_rows, group_ids, group_live = pieces
        picked = jnp.take(bank_blocks, group_ids, axis=0)
        queries = group_rows.reshape(group_slots, TB, embed_width)
        scores = (
            logit_scale
            * jnp.einsum("gte,gbe->gtb", queries, picked, preferred_element_type=jnp.float32)
            + logit_bias
        )
        hard_coef = (jax.nn.sigmoid(scores) * group_live[:, None, None]).astype(jnp.bfloat16)
        result = logit_scale * jnp.einsum(
            "gtb,gbe->gte", hard_coef, picked, preferred_element_type=jnp.float32
        )
        return result.astype(jnp.bfloat16).reshape(group_slots, TB * embed_width)

    answers = lax.map(
        per_group,
        (
            incoming.reshape(groups, group_slots, -1),
            safe_ids.reshape(groups, group_slots),
            live_slots.reshape(groups, group_slots),
        ),
    )
    return answers.reshape(slot_count, TB * embed_width)


def local(text_feats, proj, first_moment, second_moment, owners, blocks, positives, bank):
    devices = lax.axis_size(("gx", "gy"))
    weight_half = lax.all_gather(proj.astype(jnp.bfloat16), ("gx", "gy"), axis=0, tiled=True)
    projected = jnp.dot(text_feats, weight_half, preferred_element_type=jnp.float32)
    radius = jnp.sqrt(jnp.sum(projected * projected, axis=-1, keepdims=True) + norm_eps)
    unit_rows = projected / radius
    unit_half = unit_rows.astype(jnp.bfloat16)
    rows_dev = text_feats.shape[0]
    embed_width = unit_rows.shape[1]
    text_blocks = rows_dev // TB
    visits = text_blocks * HARD
    capacity = max(2, visits // devices + 1)
    slot_count = devices * capacity
    flat_owner = owners.reshape(-1)
    flat_block = blocks.reshape(-1)
    visit_order = jnp.arange(visits, dtype=jnp.int32)
    same_owner = (flat_owner[:, None] == flat_owner[None, :]) & (
        visit_order[None, :] < visit_order[:, None]
    )
    earlier = jnp.sum(same_owner.astype(jnp.int32), axis=1)
    slot_index = flat_owner * capacity + earlier
    placement = jnp.arange(slot_count, dtype=jnp.int32)[:, None] == slot_index[None, :]
    visit_block = (
        (visit_order // HARD)[:, None] == jnp.arange(text_blocks, dtype=jnp.int32)[None, :]
    ).astype(jnp.bfloat16)
    select = jnp.dot(
        placement.astype(jnp.bfloat16), visit_block, preferred_element_type=jnp.float32
    ).astype(jnp.bfloat16)
    block_tags = (jnp.sum(jnp.where(placement, flat_block[None, :] + 1, 0), axis=1) - 1).astype(
        jnp.bfloat16
    )
    outgoing = jnp.dot(
        select, unit_half.reshape(text_blocks, TB * embed_width), preferred_element_type=jnp.float32
    ).astype(jnp.bfloat16)
    arrived = (
        lax.all_to_all(outgoing, ("gx", "gy"), split_axis=0, concat_axis=0, tiled=True),
        lax.all_to_all(block_tags, ("gx", "gy"), split_axis=0, concat_axis=0, tiled=True),
    )
    replies = answer_visits(arrived[0], arrived[1], bank)
    returned = lax.all_to_all(replies, ("gx", "gy"), split_axis=0, concat_axis=0, tiled=True)
    scores = (
        logit_scale * jnp.dot(unit_half, bank.T, preferred_element_type=jnp.float32) + logit_bias
    )
    columns = jnp.arange(bank.shape[0], dtype=jnp.int32)
    labels = jnp.where(columns[None, :] == positives[:, None], 1.0, -1.0).astype(jnp.float32)
    local_coef = (-labels * jax.nn.sigmoid(-labels * scores)).astype(jnp.bfloat16)
    local_grad = logit_scale * jnp.dot(local_coef, bank, preferred_element_type=jnp.float32)
    visit_sum = jnp.dot(select.T, returned, preferred_element_type=jnp.float32).reshape(
        rows_dev, embed_width
    )
    embed_grad = local_grad + visit_sum
    radial = jnp.sum(unit_rows * embed_grad, axis=-1, keepdims=True)
    proj_grad_rows = ((embed_grad - unit_rows * radial) / radius).astype(jnp.bfloat16)
    text_grad = jnp.dot(proj_grad_rows, weight_half.T, preferred_element_type=jnp.float32).astype(
        jnp.bfloat16
    )
    weight_grad = lax.psum_scatter(
        lax.dot_general(
            text_feats, proj_grad_rows, (((0,), (0,)), ((), ())), preferred_element_type=jnp.float32
        ),
        ("gx", "gy"),
        scatter_dimension=0,
        tiled=True,
    )
    new_first = beta_one * first_moment + (1.0 - beta_one) * weight_grad
    new_second = beta_two * second_moment + (1.0 - beta_two) * weight_grad * weight_grad
    first_hat = new_first / (1.0 - beta_one**adam_step)
    second_hat = new_second / (1.0 - beta_two**adam_step)
    new_proj = proj - learn_rate * (
        first_hat / (jnp.sqrt(second_hat) + adam_eps) + decay_rate * proj
    )
    return (text_grad, new_proj, new_first, new_second)


def solution(mesh):
    return jax.shard_map(
        local,
        mesh=mesh,
        in_specs=(
            P(("gx", "gy"), None),
            P(("gx", "gy"), None),
            P(("gx", "gy"), None),
            P(("gx", "gy"), None),
            P(("gx", "gy"), None),
            P(("gx", "gy"), None),
            P(("gx", "gy")),
            P(("gx", "gy"), None),
        ),
        out_specs=(
            P(("gx", "gy"), None),
            P(("gx", "gy"), None),
            P(("gx", "gy"), None),
            P(("gx", "gy"), None),
        ),
        check_vma=False,
    )
```

profile of v0, /device:TPU:0, one launch (start us, length us, event | category | flops | bytes accessed | tf_op | source)
XLA Modules:
  0.0 996.4 jit_solution(12530511870403457518)
XLA Ops:
  7.2 1.7 convert_bitcast_fusion
  11.8 7.3 all-to-all-start.1
  20.0 53.0 %all-gather.3.cloned.1.call-done = bf16[32,36,1152]{2,1,0:T(8,128)(2,1)} async-done(((bf16[1,36,1152]{2,1,0:T(8,128)(2,1)}), bf16[32,36,1152]{2,1,0:T(8,128)(2,1)}) %all-gather.3.cloned.1.call-update) | async-done | bytes 2654224 | tf_op jit(solution)/shard_map/all_gather | solution.py:60
  72.9 5.2 reshape.156
  78.1 3.7 multiply_reduce_fusion.1
  81.8 1.5 copy-done.1
  84.2 5.7 convolution_convert_fusion
  89.8 9.6 all_to_all.18
  99.4 3.7 all-to-all-start
  103.5 212.1 %all-to-all-done = bf16[32,6,18432]{2,1,0:T(8,128)(2,1)} async-done(((bf16[32,6,18432]{2,1,0:T(8,128)(2,1)}), bf16[32,6,18432]{2,1,0:T(8,128)(2,1)}, u32[]{:S(2)}, u32[]{:S(2)}) %all-to-all-start) | async-done | bytes 7077920 | tf_op jit(solution)/shard_map/all_to_all | solution.py:93
  315.6 9.7 reshape.143
  325.3 252.8 %while.10 = (s32[]{:T(128)}, bf16[12,16,18432]{2,1,0:T(8,128)(2,1)}, bf16[12,16,18432]{2,1,0:T(8,128)(2,1)}, s32[12,16]{1,0:T(8,128)S(1)}, bf16[12,256,1152]{2,1...) while((s32[]{:T(128)}, bf16[12,16,18432]{2,1,0:T(8,128)(2,1)}, bf16[12,16,18432]{2,1,0:T(8,128)(2,1)}, ...), condition=%wide.region_4.5_spmd, body=%wide.region_3.4_spmd.sunk | while | flops 312476832 | bytes 34215036 | solution.py:47
  325.3 8.4 gather_fusion
  333.7 1.1 constant_dynamic-slice_fusion.5
  334.9 10.3 %fusion.58 = bf16[16,16,1152]{2,1,0:T(8,128)(2,1)S(1)} fusion(bf16[16,256,1152]{2,1,0:T(8,128)(2,1)} %gather_fusion, pred[16]{0:T(512)(128)(4,1)S(1)} %compare_and_fusion.2, bf16[16,16,1152]{2,1,0:T(8,128)(2,1)S(1)} %bitcast.48, f32[16]{0:T(128)S(1)} %fusion.57), kind=kOutput, calls=%fused_computation.5.clone.1 | convolution fusion | flops 312475648 | bytes 10616912 | tf_op jit(solution)/shard_map/while/body/eval_jaxpr/gtb,gbe->gte/dot_general | solution.py:42
  346.4 8.3 gather_fusion
  354.8 1.1 constant_dynamic-slice_fusion.5
  356.0 10.3 %fusion.58 = bf16[16,16,1152]{2,1,0:T(8,128)(2,1)S(1)} fusion(bf16[16,256,1152]{2,1,0:T(8,128)(2,1)} %gather_fusion, pred[16]{0:T(512)(128)(4,1)S(1)} %compare_and_fusion.2, bf16[16,16,1152]{2,1,0:T(8,128)(2,1)S(1)} %bitcast.48, f32[16]{0:T(128)S(1)} %fusion.57), kind=kOutput, calls=%fused_computation.5.clone.1 | convolution fusion | flops 312475648 | bytes 10616912 | tf_op jit(solution)/shard_map/while/body/eval_jaxpr/gtb,gbe->gte/dot_general | solution.py:42
  367.5 8.4 gather_fusion
  375.9 1.1 constant_dynamic-slice_fusion.5
  377.1 10.3 %fusion.58 = bf16[16,16,1152]{2,1,0:T(8,128)(2,1)S(1)} fusion(bf16[16,256,1152]{2,1,0:T(8,128)(2,1)} %gather_fusion, pred[16]{0:T(512)(128)(4,1)S(1)} %compare_and_fusion.2, bf16[16,16,1152]{2,1,0:T(8,128)(2,1)S(1)} %bitcast.48, f32[16]{0:T(128)S(1)} %fusion.57), kind=kOutput, calls=%fused_computation.5.clone.1 | convolution fusion | flops 312475648 | bytes 10616912 | tf_op jit(solution)/shard_map/while/body/eval_jaxpr/gtb,gbe->gte/dot_general | solution.py:42
  388.6 8.3 gather_fusion
  396.9 1.1 constant_dynamic-slice_fusion.5
  398.1 10.3 %fusion.58 = bf16[16,16,1152]{2,1,0:T(8,128)(2,1)S(1)} fusion(bf16[16,256,1152]{2,1,0:T(8,128)(2,1)} %gather_fusion, pred[16]{0:T(512)(128)(4,1)S(1)} %compare_and_fusion.2, bf16[16,16,1152]{2,1,0:T(8,128)(2,1)S(1)} %bitcast.48, f32[16]{0:T(128)S(1)} %fusion.57), kind=kOutput, calls=%fused_computation.5.clone.1 | convolution fusion | flops 312475648 | bytes 10616912 | tf_op jit(solution)/shard_map/while/body/eval_jaxpr/gtb,gbe->gte/dot_general | solution.py:42
  409.6 8.3 gather_fusion
  418.0 1.1 constant_dynamic-slice_fusion.5
  419.2 10.3 %fusion.58 = bf16[16,16,1152]{2,1,0:T(8,128)(2,1)S(1)} fusion(bf16[16,256,1152]{2,1,0:T(8,128)(2,1)} %gather_fusion, pred[16]{0:T(512)(128)(4,1)S(1)} %compare_and_fusion.2, bf16[16,16,1152]{2,1,0:T(8,128)(2,1)S(1)} %bitcast.48, f32[16]{0:T(128)S(1)} %fusion.57), kind=kOutput, calls=%fused_computation.5.clone.1 | convolution fusion | flops 312475648 | bytes 10616912 | tf_op jit(solution)/shard_map/while/body/eval_jaxpr/gtb,gbe->gte/dot_general | solution.py:42
  430.7 8.3 gather_fusion
  439.0 1.1 constant_dynamic-slice_fusion.5
  440.2 10.3 %fusion.58 = bf16[16,16,1152]{2,1,0:T(8,128)(2,1)S(1)} fusion(bf16[16,256,1152]{2,1,0:T(8,128)(2,1)} %gather_fusion, pred[16]{0:T(512)(128)(4,1)S(1)} %compare_and_fusion.2, bf16[16,16,1152]{2,1,0:T(8,128)(2,1)S(1)} %bitcast.48, f32[16]{0:T(128)S(1)} %fusion.57), kind=kOutput, calls=%fused_computation.5.clone.1 | convolution fusion | flops 312475648 | bytes 10616912 | tf_op jit(solution)/shard_map/while/body/eval_jaxpr/gtb,gbe->gte/dot_general | solution.py:42
  450.9 0.9 constant_dynamic-update-slice_fusion.2
  451.8 8.3 gather_fusion
  460.1 1.1 constant_dynamic-slice_fusion.5
  461.3 10.3 %fusion.58 = bf16[16,16,1152]{2,1,0:T(8,128)(2,1)S(1)} fusion(bf16[16,256,1152]{2,1,0:T(8,128)(2,1)} %gather_fusion, pred[16]{0:T(512)(128)(4,1)S(1)} %compare_and_fusion.2, bf16[16,16,1152]{2,1,0:T(8,128)(2,1)S(1)} %bitcast.48, f32[16]{0:T(128)S(1)} %fusion.57), kind=kOutput, calls=%fused_computation.5.clone.1 | convolution fusion | flops 312475648 | bytes 10616912 | tf_op jit(solution)/shard_map/while/body/eval_jaxpr/gtb,gbe->gte/dot_general | solution.py:42
  472.8 8.4 gather_fusion
  481.2 1.1 constant_dynamic-slice_fusion.5
  482.4 10.3 %fusion.58 = bf16[16,16,1152]{2,1,0:T(8,128)(2,1)S(1)} fusion(bf16[16,256,1152]{2,1,0:T(8,128)(2,1)} %gather_fusion, pred[16]{0:T(512)(128)(4,1)S(1)} %compare_and_fusion.2, bf16[16,16,1152]{2,1,0:T(8,128)(2,1)S(1)} %bitcast.48, f32[16]{0:T(128)S(1)} %fusion.57), kind=kOutput, calls=%fused_computation.5.clone.1 | convolution fusion | flops 312475648 | bytes 10616912 | tf_op jit(solution)/shard_map/while/body/eval_jaxpr/gtb,gbe->gte/dot_general | solution.py:42
  493.9 8.3 gather_fusion
  502.3 1.1 constant_dynamic-slice_fusion.5
  503.5 10.3 %fusion.58 = bf16[16,16,1152]{2,1,0:T(8,128)(2,1)S(1)} fusion(bf16[16,256,1152]{2,1,0:T(8,128)(2,1)} %gather_fusion, pred[16]{0:T(512)(128)(4,1)S(1)} %compare_and_fusion.2, bf16[16,16,1152]{2,1,0:T(8,128)(2,1)S(1)} %bitcast.48, f32[16]{0:T(128)S(1)} %fusion.57), kind=kOutput, calls=%fused_computation.5.clone.1 | convolution fusion | flops 312475648 | bytes 10616912 | tf_op jit(solution)/shard_map/while/body/eval_jaxpr/gtb,gbe->gte/dot_general | solution.py:42
  515.0 8.3 gather_fusion
  523.3 1.1 constant_dynamic-slice_fusion.5
  524.5 10.3 %fusion.58 = bf16[16,16,1152]{2,1,0:T(8,128)(2,1)S(1)} fusion(bf16[16,256,1152]{2,1,0:T(8,128)(2,1)} %gather_fusion, pred[16]{0:T(512)(128)(4,1)S(1)} %compare_and_fusion.2, bf16[16,16,1152]{2,1,0:T(8,128)(2,1)S(1)} %bitcast.48, f32[16]{0:T(128)S(1)} %fusion.57), kind=kOutput, calls=%fused_computation.5.clone.1 | convolution fusion | flops 312475648 | bytes 10616912 | tf_op jit(solution)/shard_map/while/body/eval_jaxpr/gtb,gbe->gte/dot_general | solution.py:42
  536.0 8.3 gather_fusion
  544.3 1.1 constant_dynamic-slice_fusion.5
  545.5 10.3 %fusion.58 = bf16[16,16,1152]{2,1,0:T(8,128)(2,1)S(1)} fusion(bf16[16,256,1152]{2,1,0:T(8,128)(2,1)} %gather_fusion, pred[16]{0:T(512)(128)(4,1)S(1)} %compare_and_fusion.2, bf16[16,16,1152]{2,1,0:T(8,128)(2,1)S(1)} %bitcast.48, f32[16]{0:T(128)S(1)} %fusion.57), kind=kOutput, calls=%fused_computation.5.clone.1 | convolution fusion | flops 312475648 | bytes 10616912 | tf_op jit(solution)/shard_map/while/body/eval_jaxpr/gtb,gbe->gte/dot_general | solution.py:42
  556.1 0.9 constant_dynamic-update-slice_fusion.2
  557.0 8.3 gather_fusion
  565.3 1.1 constant_dynamic-slice_fusion.5
  566.5 10.3 %fusion.58 = bf16[16,16,1152]{2,1,0:T(8,128)(2,1)S(1)} fusion(bf16[16,256,1152]{2,1,0:T(8,128)(2,1)} %gather_fusion, pred[16]{0:T(512)(128)(4,1)S(1)} %compare_and_fusion.2, bf16[16,16,1152]{2,1,0:T(8,128)(2,1)S(1)} %bitcast.48, f32[16]{0:T(128)S(1)} %fusion.57), kind=kOutput, calls=%fused_computation.5.clone.1 | convolution fusion | flops 312475648 | bytes 10616912 | tf_op jit(solution)/shard_map/while/body/eval_jaxpr/gtb,gbe->gte/dot_general | solution.py:42
  577.2 0.9 constant_dynamic-update-slice_fusion.2
  578.1 9.6 all_to_all.21
  587.7 210.9 %all_to_all.27 = bf16[32,6,18432]{2,1,0:T(8,128)(2,1)} all-to-all(bf16[32,6,18432]{2,1,0:T(8,128)(2,1)} %all_to_all.21), channel_id=1, replica_groups=mesh['gx'=4,'gy'=8] {'gx','gy'}, dimensions={0} | all-to-all | bytes 14155776 | tf_op jit(solution)/shard_map/all_to_all | solution.py:97
  798.6 9.7 all_to_all.23
  808.3 5.9 fusion.37
  814.2 3.0 reshape.145
  817.2 16.0 %multiply_reduce_fusion = (f32[512]{0:T(512)S(1)}, f32[512,1152]{1,0:T(8,128)}) fusion(f32[512,1152]{1,0:T(8,128)S(1)} %copy-done.2, f32[512]{0:T(512)S(1)} %copy-done.10, f32[512,1152]{1,0:T(8,128)} %reshape.145, bf16[3072,1152]{1,0:T(8,128)(2,1)} %bitcast.46, s32[512]{0:T(512)S(1)} %copy-done.11), kind=kOutput, calls=%fused_computation.40 | convolution fusion | flops 7269187072 | bytes 14161920 | tf_op jit(solution)/shard_map/dot_general | solution.py:104
  833.3 2.1 divide_convert_fusion
  835.4 1.0 copy-done.3
  836.4 4.1 convolution_bitcast_fusion
  840.5 1.2 copy-done.4
  841.8 4.7 convolution_convert_fusion.1
  846.5 140.4 %all-reduce.3.cloned.1.call-done = f32[1152,1152]{0,1:T(8,128)} async-done(((f32[1152,1152]{0,1:T(8,128)}), f32[1152,1152]{0,1:T(8,128)}) %all-reduce.3.cloned.1.call-update) | async-done | bytes 5308432
  986.9 1.5 constant_dynamic-slice_fusion.3
  (128 shorter events, 18.4 us)
Async XLA Ops:
  7.2 71.0 %copy-start = (bf16[512,1152]{1,0:T(8,128)(2,1)S(1)}, bf16[512,1152]{1,0:T(8,128)(2,1)}, u32[]{:S(2)}) copy-start(bf16[512,1152]{1,0:T(8,128)(2,1)} %param.10) | copy-start | bytes 3538948
  7.2 65.8 %all-gather.3.cloned.1.call-start = ((), (), s32[]{:S(2)}) async-start(), calls=%async_computation.3 | async-start | bytes 3041280 | tf_op jit(solution)/shard_map/all_gather | solution.py:60
  11.8 87.7 %all-to-all-start.1 = ((bf16[32,6,1]{1,2,0:T(2,128)(2,1)}), bf16[32,6,1]{1,2,0:T(2,128)(2,1)S(1)}, u32[]{:S(2)}, u32[]{:S(2)}) async-start(bf16[32,6,1]{1,2,0:T(2,128)(2,1)} %convert_element_type.72), calls=%async_computation.1 | async-start | bytes 32768 | tf_op jit(solution)/shard_map/all_to_all | solution.py:94
  81.8 1.5 copy-start.1
  81.8 1.5 copy-start.9
  99.4 216.2 %all-to-all-start = ((bf16[32,6,18432]{2,1,0:T(8,128)(2,1)}), bf16[32,6,18432]{2,1,0:T(8,128)(2,1)}, u32[]{:S(2)}, u32[]{:S(2)}) async-start(bf16[32,6,18432]{2,1,0:T(8,128)(2,1)} %all_to_all.18), calls=%async_computation | async-start | bytes 18874368 | tf_op jit(solution)/shard_map/all_to_all | solution.py:93
  103.1 883.8 %all-reduce.3.cloned.1.call-start = ((), (), s32[]{:S(2)}) async-start(), calls=%async_computation.4 | async-start | bytes 10616832
  798.6 9.7 copy-start.8
  814.2 3.0 copy-start.2
  814.2 3.0 copy-start.10
  814.2 3.0 copy-start.11
  835.4 1.0 copy-start.3
  840.5 1.3 copy-start.4
  841.8 146.9 %copy-start.5 = (f32[36,1152]{1,0:T(8,128)S(1)}, f32[36,1152]{1,0:T(8,128)}, u32[]{:S(2)}) copy-start(f32[36,1152]{1,0:T(8,128)} %param.11) | copy-start | bytes 497668
  841.8 146.9 %copy-start.6 = (f32[36,1152]{1,0:T(8,128)S(1)}, f32[36,1152]{1,0:T(8,128)}, u32[]{:S(2)}) copy-start(f32[36,1152]{1,0:T(8,128)} %param.12) | copy-start | bytes 497668
  841.8 146.9 %copy-start.7 = (f32[36,1152]{1,0:T(8,128)S(1)}, f32[36,1152]{1,0:T(8,128)}, u32[]{:S(2)}) copy-start(f32[36,1152]{1,0:T(8,128)} %param.13) | copy-start | bytes 497668
Sparse Core Ops, SparseCore 0:
  11.4 61.4 all-gather.2
  840.6 146.2 all-reduce.2
where the time goes:
time: 999 us; the launch traced here: 996 us
  waiting for transfers between devices  406 us (41%)
  blocking collectives  211 us (21%)
  local copies, waits for them, and re-layouts  183 us (18%)
  matrix products  165 us (17%)
  between operations  14.2 us (1%)
  starting transfers between devices  11.1 us (1%)
    all_to_all x1, waiting for transfers between devices, local(): lax.all_to_all(outgoing, ('gx', 'gy'), split_axis=0, concat_axis=0, tiled...  212 us
    all_to_all x1, blocking collectives, local(): lax.all_to_all(replies, ('gx', 'gy'), split_axis=0, concat_axis=0, tiled=...  211 us
    unnamed x3, waiting for transfers between devices  140 us
    dot_general x12, matrix products, per_group(): jnp.einsum('gtb,gbe->gte', hard_coef, picked, preferred_element_type=jnp....  124 us
    gather x12, local copies, waits for them, and re-layouts, per_group(): picked = jnp.take(bank_blocks, group_ids, axis=0)  100 us
    all_gather x1, waiting for transfers between devices, local(): lax.all_gather(proj.astype(jnp.bfloat16), ('gx', 'gy'), axis=0, tiled=True)  53 us
  transfers between devices with their start and end apart: 4, of which 3 were waited for; matrix products, arithmetic and copies ran while one was open for 2% of the time, Pallas kernels for 0%

commit v1 on v0

v1 whole, which is shorter than its diff:
```python
import functools

import jax
import jax.numpy as jnp
from jax import lax
from jax.experimental import pallas as pl
from jax.experimental.pallas import tpu as pltpu
from jax.sharding import Mesh, PartitionSpec as P

BROWS = 256
TILE_SLOTS = 8

logit_scale = 20.0
logit_bias = -3.0
norm_eps = 1e-06
beta_one = 0.9
beta_two = 0.999
learn_rate = 0.001
decay_rate = 0.1
adam_eps = 1e-08
adam_step = 100.0

ALL = ("x", "c", "zh", "zl", "y")
PLANE = ("x", "c", "y")
COLUMN = ("zh", "zl")
SWAP = [(0, 1), (1, 0)]
bf16 = jnp.bfloat16
f32 = jnp.float32


def answer_kernel(
    slots, tb, banks, row_chunk, tags_ref, x_ref, w_hbm, bank_hbm, out_ref,
    w_ref, bank_ref, unit_ref, order_ref, count_ref, tile_bank, tile_first, tile_last, sems,
):
    w_copy = pltpu.make_async_copy(w_hbm, w_ref, sems.at[0])
    bank_copy = pltpu.make_async_copy(bank_hbm, bank_ref, sems.at[1])
    w_copy.start()
    bank_copy.start()

    for b in range(banks):
        count_ref[b] = 0

    def count(s, carry):
        b = tags_ref[s]
        count_ref[b] = count_ref[b] + 1
        return carry

    lax.fori_loop(0, slots, count, 0)

    def lay(b, carry):
        first, tiles = carry
        n = count_ref[b]
        last = first + n - 1

        def tile(i, carry):
            tile_bank[tiles + i] = b
            tile_first[tiles + i] = first + i * TILE_SLOTS
            tile_last[tiles + i] = last
            return carry

        n_tiles = lax.div(n + TILE_SLOTS - 1, TILE_SLOTS)
        lax.fori_loop(0, n_tiles, tile, 0)
        count_ref[b] = first
        return first + n, tiles + n_tiles

    _, n_tiles = lax.fori_loop(0, banks, lay, (0, 0))

    def place(s, carry):
        b = tags_ref[s]
        at = count_ref[b]
        order_ref[at] = s
        count_ref[b] = at + 1
        return carry

    lax.fori_loop(0, slots, place, 0)

    w_copy.wait()

    def project(i, carry):
        rows = pl.ds(pl.multiple_of(i * row_chunk, row_chunk), row_chunk)
        projected = jnp.dot(x_ref[rows, :], w_ref[...], preferred_element_type=f32)
        radius = jnp.sqrt(jnp.sum(projected * projected, axis=-1, keepdims=True) + norm_eps)
        unit_ref[rows, :] = (projected * (1.0 / radius)).astype(bf16)
        return carry

    lax.fori_loop(0, slots * tb // row_chunk, project, 0)
    bank_copy.wait()

    def answer(t, carry):
        b = tile_bank[t]
        first = tile_first[t]
        last = tile_last[t]
        at = []
        for i in range(TILE_SLOTS):
            at.append(pl.multiple_of(order_ref[jnp.minimum(first + i, last)] * tb, tb))
        queries = jnp.concatenate([unit_ref[pl.ds(a, tb), :] for a in at], axis=0)
        keys = bank_ref[pl.ds(pl.multiple_of(b * BROWS, BROWS), BROWS), :]
        scores = lax.dot_general(queries, keys, (((1,), (1,)), ((), ())), preferred_element_type=f32)
        coef = jax.nn.sigmoid(logit_scale * scores + logit_bias).astype(bf16)
        grad = logit_scale * jnp.dot(coef, keys, preferred_element_type=f32)
        grad = grad.astype(bf16)
        for i, a in enumerate(at):
            out_ref[pl.ds(a, tb), :] = grad[i * tb : (i + 1) * tb, :]
        return carry

    lax.fori_loop(0, n_tiles, answer, 0)


def answer(x, tags, weight_half, bank, tb):
    rows, width = x.shape
    slots = rows // tb
    banks = bank.shape[0] // BROWS
    most_tiles = slots // TILE_SLOTS + banks + 1
    row_chunk = 256 if rows % 256 == 0 else tb
    return pl.pallas_call(
        functools.partial(answer_kernel, slots, tb, banks, row_chunk),
        out_shape=jax.ShapeDtypeStruct((rows, bank.shape[1]), bf16),
        in_specs=[
            pl.BlockSpec(memory_space=pltpu.SMEM),
            pl.BlockSpec(memory_space=pltpu.VMEM),
            pl.BlockSpec(memory_space=pl.ANY),
            pl.BlockSpec(memory_space=pl.ANY),
        ],
        out_specs=pl.BlockSpec(memory_space=pltpu.VMEM),
        scratch_shapes=[
            pltpu.VMEM(weight_half.shape, bf16),
            pltpu.VMEM(bank.shape, bf16),
            pltpu.VMEM((rows, bank.shape[1]), bf16),
            pltpu.SMEM((slots,), jnp.int32),
            pltpu.SMEM((banks,), jnp.int32),
            pltpu.SMEM((most_tiles,), jnp.int32),
            pltpu.SMEM((most_tiles,), jnp.int32),
            pltpu.SMEM((most_tiles,), jnp.int32),
            pltpu.SemaphoreType.DMA((2,)),
        ],
        compiler_params=pltpu.CompilerParams(vmem_limit_bytes=40 << 20),
        cost_estimate=pl.CostEstimate(
            flops=2 * rows * width * width + 8 * rows * width * BROWS,
            bytes_accessed=4 * rows * width + 2 * width * width + 2 * bank.size,
            transcendentals=rows * BROWS,
        ),
        name="answer",
    )(tags, x, weight_half, bank)


def route(owners, blocks, capacity, tb):
    n_blocks, hard = owners.shape
    visits = n_blocks * hard
    n_x, n_c, n_h, n_l, n_y = (lax.axis_size(a) for a in ALL)
    x, c, zh, zl, y = (lax.axis_index(a) for a in ALL)
    devices = n_x * n_c * n_h * n_l * n_y
    pad = -(2 * visits) % 1024
    own = jnp.concatenate([owners.reshape(-1), blocks.reshape(-1), jnp.zeros((pad,), jnp.int32)])
    table = jnp.broadcast_to(own.reshape(1, -1, 128), (devices, own.shape[0] // 128, 128))
    table = lax.all_to_all(table, ALL, split_axis=0, concat_axis=0, tiled=True)
    table = table.reshape(n_x, n_c, n_h, n_l, n_y, -1)
    table = jnp.where(zh == 0, table, jnp.flip(table, 2))
    table = jnp.where(zl == 0, table, jnp.flip(table, 3))
    table = table.transpose(2, 3, 0, 1, 4, 5).reshape(n_h * n_l, n_x * n_c * n_y, -1)
    plane_at = (x * n_c + c) * n_y + y
    mine = lax.dynamic_index_in_dim(table, plane_at, 1, keepdims=False)[:, None, :visits]
    xs, cs, ys = jnp.arange(n_x), jnp.arange(n_c), jnp.arange(n_y)
    z_at = zh * n_l + zl
    dest = (((xs[:, None, None] * n_c + cs[None, :, None]) * (n_h * n_l)) + z_at) * n_y + ys[None, None, :]
    me = ((x * n_c + c) * (n_h * n_l) + z_at) * n_y + y
    sent = mine == dest.reshape(1, -1, 1)
    got = table[:, :, :visits] == me
    both = jnp.stack([sent, got])
    order = jnp.arange(visits, dtype=jnp.int32)
    before = (order[:, None] < order[None, :]).astype(bf16)
    rank = jnp.dot(both.astype(bf16), before, preferred_element_type=f32)
    values = jnp.stack([jnp.broadcast_to(order // hard + 1, got.shape), table[:, :, visits : 2 * visits] + 1])
    hit = both[..., None, :] & (rank[..., None, :] == jnp.arange(capacity, dtype=f32)[:, None])
    picked = jnp.sum(jnp.where(hit, values[..., None, :], 0), axis=-1) - 1
    picked = picked.reshape(2, n_h * n_l, -1)
    return picked[0], jnp.maximum(picked[1], 0)


def gather_weight(proj):
    n_x, n_c, n_h, n_l, n_y = (lax.axis_size(a) for a in ALL)
    rows, width = proj.shape
    piece = proj.astype(bf16)[None]
    n_z = n_h * n_l
    piece = lax.all_to_all(jnp.broadcast_to(piece, (n_z, rows, width)), COLUMN, split_axis=0, concat_axis=0, tiled=True)
    piece = jnp.broadcast_to(piece[None], (n_x * n_y, n_z, rows, width))
    piece = lax.all_to_all(piece, ("x", "y"), split_axis=0, concat_axis=0, tiled=True)
    other = lax.ppermute(piece, "c", SWAP)
    low = lax.axis_index("c") == 0
    both = jnp.stack([jnp.where(low, piece, other), jnp.where(low, other, piece)])
    both = both.reshape(n_c, n_x, n_y, n_z, rows, width).transpose(1, 0, 3, 2, 4, 5)
    return both.reshape(-1, width)


def reduce_weight(grad):
    n_x, n_c, n_h, n_l, n_y = (lax.axis_size(a) for a in ALL)
    width = grad.shape[1]
    n_z = n_h * n_l
    rows = grad.shape[0] // (n_x * n_c * n_z * n_y)
    grad = grad.reshape(n_x, n_c, n_z * n_y * rows, width)
    c = lax.axis_index("c")
    send = lax.dynamic_index_in_dim(grad, 1 - c, 1, keepdims=False).astype(bf16)
    keep = lax.dynamic_index_in_dim(grad, c, 1, keepdims=False)
    total = keep + lax.ppermute(send, "c", SWAP).astype(f32)
    total = total.reshape(n_x, n_z, n_y, rows, width).transpose(0, 2, 1, 3, 4)
    total = total.reshape(n_x * n_y, n_z * rows, width).astype(bf16)
    total = lax.all_to_all(total, ("x", "y"), split_axis=0, concat_axis=0, tiled=True)
    total = jnp.sum(total.astype(f32), axis=0).reshape(n_z, rows, width).astype(bf16)
    total = lax.all_to_all(total, COLUMN, split_axis=0, concat_axis=0, tiled=True)
    return jnp.sum(total.astype(f32), axis=0)


def local(text_feats, proj, first_moment, second_moment, owners, blocks, positives, bank):
    devices = lax.axis_size(ALL)
    plane = lax.axis_size(PLANE)
    rows_dev, width = text_feats.shape
    text_blocks, hard = owners.shape
    tb = rows_dev // text_blocks
    visits = text_blocks * hard
    capacity = max(2, visits // devices + 1)
    embed_width = bank.shape[1]

    text_low = lax.ppermute(text_feats, "zl", SWAP)
    text_high = lax.ppermute(text_feats, "zh", SWAP)
    text_far = lax.ppermute(text_high, "zl", SWAP)
    texts = (text_feats, text_low, text_high, text_far)
    sources, tags = route(owners, blocks, capacity, tb)
    weight_half = gather_weight(proj)

    def exchange(rows):
        rows = rows.reshape(plane, capacity * tb, -1)
        rows = lax.all_to_all(rows, PLANE, split_axis=0, concat_axis=0, tiled=True)
        return rows.reshape(plane * capacity * tb, -1)

    partial = []
    for k in range(4):
        row_of = sources[k][:, None] * tb + jnp.arange(tb, dtype=jnp.int32)[None, :]
        row_of = jnp.where(sources[k][:, None] >= 0, row_of, -1).reshape(-1)
        pick = (row_of[:, None] == jnp.arange(rows_dev, dtype=jnp.int32)[None, :]).astype(bf16)
        sent = jnp.dot(pick, texts[k], preferred_element_type=f32).astype(bf16)
        replies = exchange(answer(exchange(sent), tags[k], weight_half, bank, tb))
        partial.append(
            lax.dot_general(pick, replies, (((0,), (0,)), ((), ())), preferred_element_type=f32)
        )
    from_far = lax.ppermute(partial[3].astype(bf16), "zl", SWAP)
    from_high = lax.ppermute((partial[2] + from_far.astype(f32)).astype(bf16), "zh", SWAP)
    from_low = lax.ppermute(partial[1].astype(bf16), "zl", SWAP)
    visit_sum = partial[0] + from_low.astype(f32) + from_high.astype(f32)

    projected = jnp.dot(text_feats, weight_half, preferred_element_type=f32)
    radius = jnp.sqrt(jnp.sum(projected * projected, axis=-1, keepdims=True) + norm_eps)
    unit_rows = projected / radius
    unit_half = unit_rows.astype(bf16)
    scores = logit_scale * jnp.dot(unit_half, bank.T, preferred_element_type=f32) + logit_bias
    columns = jnp.arange(bank.shape[0], dtype=jnp.int32)
    labels = jnp.where(columns[None, :] == positives[:, None], 1.0, -1.0).astype(f32)
    local_coef = (-labels * jax.nn.sigmoid(-labels * scores)).astype(bf16)
    local_grad = logit_scale * jnp.dot(local_coef, bank, preferred_element_type=f32)

    embed_grad = local_grad + visit_sum
    radial = jnp.sum(unit_rows * embed_grad, axis=-1, keepdims=True)
    proj_grad_rows = ((embed_grad - unit_rows * radial) / radius).astype(bf16)
    weight_grad = reduce_weight(
        lax.dot_general(text_feats, proj_grad_rows, (((0,), (0,)), ((), ())), preferred_element_type=f32)
    )
    text_grad = jnp.dot(proj_grad_rows, weight_half.T, preferred_element_type=f32).astype(bf16)
    new_first = beta_one * first_moment + (1.0 - beta_one) * weight_grad
    new_second = beta_two * second_moment + (1.0 - beta_two) * weight_grad * weight_grad
    first_hat = new_first / (1.0 - beta_one**adam_step)
    second_hat = new_second / (1.0 - beta_two**adam_step)
    new_proj = proj - learn_rate * (first_hat / (jnp.sqrt(second_hat) + adam_eps) + decay_rate * proj)
    return (text_grad, new_proj, new_first, new_second)


def solution(mesh):
    n_gx, n_gy = mesh.shape["gx"], mesh.shape["gy"]
    fine = Mesh(mesh.devices.reshape(n_gx // 2, 2, 2, 2, n_gy // 4), ALL)
    rows = P(ALL, None)
    return jax.shard_map(
        local,
        mesh=fine,
        in_specs=(rows, rows, rows, rows, rows, rows, P(ALL), rows),
        out_specs=(rows, rows, rows, rows),
        check_vma=False,
    )
```

time: 999 us -> 471 us (0.47)
  waiting for transfers between devices: 406 us -> 191 us
  blocking collectives: 211 us -> 22.4 us
  local copies, waits for them, and re-layouts: 183 us -> 50.7 us
  matrix products: 165 us -> 58.9 us
  Pallas kernels: 0 us -> 60.3 us
  starting transfers between devices: 11.1 us -> 57.4 us
  other arithmetic: 6.39 us -> 20.2 us
  between operations: 14.2 us -> 1.61 us
    all_to_all x1, blocking collectives: 211 us -> 22.4 us  [reduce_weight(): lax.all_to_all(total, ('x', 'y'), split_axis=0, concat_axis=0, tiled=True)]
    all_to_all x2 -> x12, waiting for transfers between devices: 212 us -> 44.8 us  [the longest x1 12.6 us: gather_weight(): lax.all_to_all(piece, ('x', 'y'), split_axis=0, concat_axis=0, tiled=True)]
    ppermute x0 -> x8, waiting for transfers between devices: none -> 146 us  [the longest x1 53 us: local(): text_high = lax.ppermute(text_feats, 'zh', SWAP)]
    unnamed x3 -> x0, waiting for transfers between devices: 140 us -> none
    dot_general x18 -> x12, matrix products: 161 us -> 57.2 us  [the longest x1 20 us: local(): jnp.dot(local_coef, bank, preferred_element_type=f32)]
    gather x12 -> x0, local copies, waits for them, and re-layouts: 100 us -> none  [per_group(): picked = jnp.take(bank_blocks, group_ids, axis=0)]
    pallas_call x0 -> x4, Pallas kernels: none -> 60.3 us  [answer(): pl.pallas_call(functools.partial(answer_kernel, slots, tb, banks, row_chu...]
    all_gather x1 -> x0, waiting for transfers between devices: 53 us -> none  [local(): lax.all_gather(proj.astype(jnp.bfloat16), ('gx', 'gy'), axis=0, tiled=True)]
  transfers between devices with their start and end apart: 4 -> 20, of which waited for: 3 -> 13; matrix products, arithmetic and copies ran while one was open for 2% -> 12% of each run, Pallas kernels for 0% -> 13%
where the time goes in v1:
time: 471 us; the launch traced here: 462 us
  waiting for transfers between devices  191 us (41%)
  Pallas kernels  60.3 us (13%)
  matrix products  58.9 us (13%)
  starting transfers between devices  57.4 us (12%)
  local copies, waits for them, and re-layouts  50.7 us (11%)
  blocking collectives  22.4 us (5%)
  other arithmetic  20.2 us (4%)
    pallas_call x4, Pallas kernels, answer(): pl.pallas_call(functools.partial(answer_kernel, slots, tb, banks, row_chu...  60.3 us
    ppermute x1, waiting for transfers between devices, local(): text_high = lax.ppermute(text_feats, 'zh', SWAP)  53 us
    all_to_all x8, starting transfers between devices, exchange(): rows = lax.all_to_all(rows, PLANE, split_axis=0, concat_axis=0, tiled=True)  33.3 us
    unnamed x52, local copies, waits for them, and re-layouts  30.5 us
    ppermute x1, waiting for transfers between devices, local(): from_low = lax.ppermute(partial[1].astype(bf16), 'zl', SWAP)  28.3 us
    ppermute x1, waiting for transfers between devices, local(): text_low = lax.ppermute(text_feats, 'zl', SWAP)  27.8 us
    ppermute x1, waiting for transfers between devices, local(): text_far = lax.ppermute(text_high, 'zl', SWAP)  26.3 us
    all_to_all x1, blocking collectives, reduce_weight(): lax.all_to_all(total, ('x', 'y'), split_axis=0, concat_axis=0, tiled=True)  22.4 us
  transfers between devices with their start and end apart: 20, of which 13 were waited for; matrix products, arithmetic and copies ran while one was open for 12% of the time, Pallas kernels for 13%

profile of v1, /device:TPU:0, one launch (start us, length us, event | category | flops | bytes accessed | tf_op | source)
XLA Modules:
  0.0 462.3 jit_solution(3438075380347623706)
XLA Ops:
  3.1 7.3 %all-to-all-start.2 = ((s32[32,8,128]{2,1,0:T(8,128)}), s32[32,8,128]{2,1,0:T(8,128)S(1)}, u32[]{:S(2)}, u32[]{:S(2)}) async-start(s32[32,8,128]{2,1,0:T(8,128)} %broadcast_in_dim.99), calls=%async_computation.2 | async-start | bytes 262144 | tf_op jit(solution)/shard_map/all_to_all | solution.py:155
  11.7 6.6 %all-to-all-done.2 = s32[32,8,128]{2,1,0:T(8,128)S(1)} async-done(((s32[32,8,128]{2,1,0:T(8,128)}), s32[32,8,128]{2,1,0:T(8,128)S(1)}, u32[]{:S(2)}, u32[]{:S(2)}) %all-to-all-start.2) | async-done | bytes 131104 | tf_op jit(solution)/shard_map/all_to_all | solution.py:155
  19.0 3.5 all-to-all-start
  24.1 10.1 %all-to-all-done = bf16[4,36,1152]{2,1,0:T(8,128)(2,1)S(1)} async-done(((bf16[4,36,1152]{2,1,0:T(8,128)(2,1)}), bf16[4,36,1152]{2,1,0:T(8,128)(2,1)S(1)}, u32[]{:S(2)}, u32[]{:S(2)}) %all-to-all-start) | async-done | bytes 331808 | tf_op jit(solution)/shard_map/all_to_all | solution.py:184
  34.3 1.4 broadcast_in_dim.96
  35.8 3.7 all-to-all-start.1
  40.6 2.5 convolution_convert_fusion.3
  43.1 12.6 %all-to-all-done.1 = bf16[4,4,36,1152]{3,1,2,0:T(4,128)(2,1)S(1)} async-done(((bf16[4,4,36,1152]{3,1,2,0:T(4,128)(2,1)}), bf16[4,4,36,1152]{3,1,2,0:T(4,128)(2,1)S(1)}, u32[]{:S(2)}, u32[]{:S(2)}) %all-to-all-start.1) | async-done | bytes 1327136 | tf_op jit(solution)/shard_map/all_to_all | solution.py:186
  56.9 3.6 all-to-all-start.3
  61.0 27.8 %collective-permute-done.1 = bf16[512,1152]{1,0:T(8,128)(2,1)} collective-permute-done((bf16[512,1152]{1,0:T(8,128)(2,1)S(1)}, bf16[512,1152]{1,0:T(8,128)(2,1)}, u32[]{:S(2)}, u32[]{:S(2)}) %collective-permute-start.1) | collective-permute-done | bytes 1179680 | tf_op jit(solution)/shard_map/ppermute | solution.py:222
  88.8 3.8 convolution_convert_fusion.2
  93.9 3.8 all-to-all-start.5
  99.2 53.0 %collective-permute-done.3 = bf16[512,1152]{1,0:T(8,128)(2,1)S(1)} collective-permute-done((bf16[512,1152]{1,0:T(8,128)(2,1)}, bf16[512,1152]{1,0:T(8,128)(2,1)S(1)}, u32[]{:S(2)}, u32[]{:S(2)}) %collective-permute-start.3) | collective-permute-done | bytes 1179680 | tf_op jit(solution)/shard_map/ppermute | solution.py:223
  152.2 2.5 convolution_convert_fusion.1
  154.8 1.3 copy-done.4
  156.1 3.8 all-to-all-start.7
  162.3 26.3 %collective-permute-done.4 = bf16[512,1152]{1,0:T(8,128)(2,1)} collective-permute-done((bf16[512,1152]{1,0:T(8,128)(2,1)}, bf16[512,1152]{1,0:T(8,128)(2,1)}, u32[]{:S(2)}, u32[]{:S(2)}) %collective-permute-start.4) | collective-permute-done | bytes 1179680 | tf_op jit(solution)/shard_map/ppermute | solution.py:224
  188.6 3.8 convolution_convert_fusion
  193.7 4.5 all-to-all-start.9
  198.3 2.0 broadcast_select_fusion.1
  200.3 1.9 maximum_bitcast_fusion
  202.2 2.0 copy.43
  204.1 3.6 reshape.342.w_hbm
  207.7 1.5 copy-done.5
  209.2 3.0 copy-done.10
  212.2 14.7 %answer.5 = bf16[768,1152]{1,0:T(8,128)(2,1)S(1)} custom-call(s32[48]{0:T(128)S(1)} %squeeze.25.tags_ref, bf16[768,1152]{1,0:T(8,128)(2,1)S(1)} %bitcast.111, bf16[1152,1152]{1,0:T(8,128)(2,1)S(1)} %reshape.342.w_hbm, bf16[3072,1152]{1,0:T(8,128)(2,1)S(1)} %copy-done.10), custom_call_target="tpu_custom_call" | custom-call | flops 3850371072 | bytes 13271040 | tf_op jit(solution)/shard_map/answer/pallas_call | solution.py:115
  228.1 4.3 all-to-all-start.6
  232.6 3.0 copy-done.11
  235.6 15.6 %answer.7 = bf16[768,1152]{1,0:T(8,128)(2,1)S(1)} custom-call(s32[48]{0:T(128)S(1)} %squeeze.27.tags_ref, bf16[768,1152]{1,0:T(8,128)(2,1)} %bitcast.23.x_ref, bf16[1152,1152]{1,0:T(8,128)(2,1)S(1)} %reshape.342.w_hbm, bf16[3072,1152]{1,0:T(8,128)(2,1)S(1)} %copy-done.11), custom_call_target="tpu_custom_call" | custom-call | flops 3850371072 | bytes 13271040 | tf_op jit(solution)/shard_map/answer/pallas_call | solution.py:115
  251.3 1.3 copy-done.9
  252.6 2.1 all-to-all-done.6
  254.7 4.3 all-to-all-start.10
  259.2 1.5 copy-done.3
  260.7 3.0 copy-done.12
  263.7 15.4 %answer.6 = bf16[768,1152]{1,0:T(8,128)(2,1)S(1)} custom-call(s32[48]{0:T(128)S(1)} %squeeze.26.tags_ref, bf16[768,1152]{1,0:T(8,128)(2,1)S(1)} %bitcast.110, bf16[1152,1152]{1,0:T(8,128)(2,1)S(1)} %reshape.342.w_hbm, bf16[3072,1152]{1,0:T(8,128)(2,1)S(1)} %copy-done.12), custom_call_target="tpu_custom_call" | custom-call | flops 3850371072 | bytes 13271040 | tf_op jit(solution)/shard_map/answer/pallas_call | solution.py:115
  281.3 4.3 all-to-all-start.8
  285.7 3.7 convolution_convert_fusion.4
  289.8 1.5 copy-done.1
  291.3 3.0 copy-done.13
  294.3 14.7 %answer.4 = bf16[768,1152]{1,0:T(8,128)(2,1)S(1)} custom-call(s32[48]{0:T(128)S(1)} %squeeze.24.tags_ref, bf16[768,1152]{1,0:T(8,128)(2,1)S(1)} %bitcast.109, bf16[1152,1152]{1,0:T(8,128)(2,1)S(1)} %reshape.342.w_hbm, bf16[3072,1152]{1,0:T(8,128)(2,1)S(1)} %copy-done.13), custom_call_target="tpu_custom_call" | custom-call | flops 3850371072 | bytes 13271040 | tf_op jit(solution)/shard_map/answer/pallas_call | solution.py:115
  310.2 4.5 all-to-all-start.4
  314.7 3.7 convolution_convert_fusion.5
  319.6 4.1 add_convert_fusion
  323.6 2.5 collective-permute-start.6
  326.1 4.4 multiply_reduce_fusion
  330.6 6.4 %all-to-all-done.4 = bf16[8,96,1152]{2,1,0:T(8,128)(2,1)} async-done(((bf16[8,96,1152]{2,1,0:T(8,128)(2,1)}), bf16[8,96,1152]{2,1,0:T(8,128)(2,1)}, u32[]{:S(2)}, u32[]{:S(2)}) %all-to-all-start.4) | async-done | bytes 1769504 | tf_op jit(solution)/shard_map/all_to_all | solution.py:231
  337.0 4.2 fusion.6
  341.1 28.3 %collective-permute-done.2 = bf16[512,1152]{0,1:T(8,128)(2,1)} collective-permute-done((bf16[512,1152]{0,1:T(8,128)(2,1)}, bf16[512,1152]{0,1:T(8,128)(2,1)}, u32[]{:S(2)}, u32[]{:S(2)}) %collective-permute-start.2) | collective-permute-done | bytes 1179680 | tf_op jit(solution)/shard_map/ppermute | solution.py:246
  369.4 9.1 %collective-permute-done.6 = bf16[512,1152]{0,1:T(8,128)(2,1)} collective-permute-done((bf16[512,1152]{0,1:T(8,128)(2,1)}, bf16[512,1152]{0,1:T(8,128)(2,1)}, u32[]{:S(2)}, u32[]{:S(2)}) %collective-permute-start.6) | collective-permute-done | bytes 1179680 | tf_op jit(solution)/shard_map/ppermute | solution.py:245
  378.5 20.0 %fusion.1 = (f32[512]{0:T(512)S(1)}, f32[512,1152]{0,1:T(8,128)}) fusion(bf16[512,1152]{0,1:T(8,128)(2,1)} %collective-permute-done.6, f32[512,1152]{0,1:T(8,128)} %fusion.6, bf16[512,1152]{0,1:T(8,128)(2,1)} %collective-permute-done.2, f32[1152,512]{1,0:T(8,128)} %get-tuple-element.22, f32[512]{0:T(512)S(1)} %add_sqrt_fusion, ...), kind=kOutput, calls=%fused_computation.17 | convolution fusion | flops 7271546368 | bytes 16521216 | tf_op jit(solution)/shard_map/dot_general | solution.py:257
  398.5 4.9 %fusion.4 = bf16[512,1152]{0,1:T(8,128)(2,1)S(1)} fusion(f32[512]{0:T(512)S(1)} %add_sqrt_fusion, f32[512]{0:T(512)S(1)} %get-tuple-element.23, f32[512,1152]{0,1:T(8,128)} %get-tuple-element.24, bf16[512,1152]{0,1:T(8,128)(2,1)} %collective-permute-done.6, f32[512,1152]{0,1:T(8,128)} %fusion.6, bf16[512,1152]{0,1:T(8,128)(2,1)} %collective-permute-done.2, ...), kind=kLoop, calls=%fused_computation.20 | loop fusion | flops 5898240 | bytes 10620928 | tf_op jit(solution)/shard_map/convert_element_type | solution.py:261
  403.5 1.7 fusion.30
  405.4 2.6 copy.79
  408.0 1.9 constant_dynamic-slice_fusion
  409.9 1.5 collective-permute-done.7
  411.4 4.1 fusion
  415.5 1.3 copy.66
  416.8 3.2 convert_element_type.101
  420.0 22.4 %all_to_all.65 = bf16[4,144,1152]{2,1,0:T(8,128)(2,1)} all-to-all(bf16[4,144,1152]{2,1,0:T(8,128)(2,1)} %convert_element_type.101), channel_id=1, replica_groups=mesh['x'=2,'c'=2,'zh'=2,'zl'=2,'y'=2] {'x','y'}, dimensions={0} | all-to-all | bytes 2654208 | tf_op jit(solution)/shard_map/all_to_all | solution.py:206
  442.4 1.5 reduce_sum.51
  444.7 5.0 %all-to-all-start.12 = ((bf16[4,36,1152]{2,1,0:T(8,128)(2,1)}), bf16[4,36,1152]{2,1,0:T(8,128)(2,1)S(1)}, u32[]{:S(2)}, u32[]{:S(2)}) async-start(bf16[4,36,1152]{2,1,0:T(8,128)(2,1)} %convert_element_type.102), calls=%async_computation.12 | async-start | bytes 737280 | tf_op jit(solution)/shard_map/all_to_all | solution.py:208
  449.7 4.2 convolution_convert_fusion.6
  454.0 6.1 %all-to-all-done.12 = bf16[4,36,1152]{2,1,0:T(8,128)(2,1)S(1)} async-done(((bf16[4,36,1152]{2,1,0:T(8,128)(2,1)}), bf16[4,36,1152]{2,1,0:T(8,128)(2,1)S(1)}, u32[]{:S(2)}, u32[]{:S(2)}) %all-to-all-start.12) | async-done | bytes 331808 | tf_op jit(solution)/shard_map/all_to_all | solution.py:208
  460.1 1.8 multiply_subtract_fusion
  (126 shorter events, 23.0 us)
Async XLA Ops:
  3.1 15.1 %all-to-all-start.2 = ((s32[32,8,128]{2,1,0:T(8,128)}), s32[32,8,128]{2,1,0:T(8,128)S(1)}, u32[]{:S(2)}, u32[]{:S(2)}) async-start(s32[32,8,128]{2,1,0:T(8,128)} %broadcast_in_dim.99), calls=%async_computation.2 | async-start | bytes 262144 | tf_op jit(solution)/shard_map/all_to_all | solution.py:155
  19.0 15.1 %all-to-all-start = ((bf16[4,36,1152]{2,1,0:T(8,128)(2,1)}), bf16[4,36,1152]{2,1,0:T(8,128)(2,1)S(1)}, u32[]{:S(2)}, u32[]{:S(2)}) async-start(bf16[4,36,1152]{2,1,0:T(8,128)(2,1)} %broadcast_in_dim.95), calls=%async_computation | async-start | bytes 737280 | tf_op jit(solution)/shard_map/all_to_all | solution.py:184
  35.8 4.8 %copy-start.20 = (bf16[512,1152]{1,0:T(8,128)(2,1)S(1)}, bf16[512,1152]{1,0:T(8,128)(2,1)}, u32[]{:S(2)}) copy-start(bf16[512,1152]{1,0:T(8,128)(2,1)} %param.8) | copy-start | bytes 3538948
  35.8 20.0 %all-to-all-start.1 = ((bf16[4,4,36,1152]{3,1,2,0:T(4,128)(2,1)}), bf16[4,4,36,1152]{3,1,2,0:T(4,128)(2,1)S(1)}, u32[]{:S(2)}, u32[]{:S(2)}) async-start(bf16[4,4,36,1152]{3,1,2,0:T(4,128)(2,1)} %broadcast_in_dim.96), calls=%async_computation.1 | async-start | bytes 2654208 | tf_op jit(solution)/shard_map/all_to_all | solution.py:186
  39.5 3.6 copy-start.18
  55.7 1.1 copy-start.14
  56.9 35.8 %all-to-all-start.3 = ((bf16[8,96,1152]{2,1,0:T(8,128)(2,1)}), bf16[8,96,1152]{2,1,0:T(8,128)(2,1)S(1)}, u32[]{:S(2)}, u32[]{:S(2)}) async-start(bf16[8,96,1152]{2,1,0:T(8,128)(2,1)} %bitcast.10), calls=%async_computation.3 | async-start | bytes 3538944 | tf_op jit(solution)/shard_map/all_to_all | solution.py:231
  60.4 28.4 %collective-permute-start.1 = (bf16[512,1152]{1,0:T(8,128)(2,1)S(1)}, bf16[512,1152]{1,0:T(8,128)(2,1)}, u32[]{:S(2)}, u32[]{:S(2)}) collective-permute-start(bf16[512,1152]{1,0:T(8,128)(2,1)S(1)} %copy-done.20), channel_id=1, source_target_pairs={{0,2},{2,0},{1,3},{3,1},{4,6},{6,4},{5,7},{7,5},{8,10},{10,8},{9,1... | collective-permute-start | bytes 3538952 | tf_op jit(solution)/shard_map/ppermute | solution.py:222
  92.7 1.2 copy-start
  93.9 60.9 %all-to-all-start.5 = ((bf16[8,96,1152]{2,1,0:T(8,128)(2,1)}), bf16[8,96,1152]{2,1,0:T(8,128)(2,1)S(1)}, u32[]{:S(2)}, u32[]{:S(2)}) async-start(bf16[8,96,1152]{2,1,0:T(8,128)(2,1)} %bitcast.123), calls=%async_computation.5 | async-start | bytes 3538944 | tf_op jit(solution)/shard_map/all_to_all | solution.py:231
  97.7 54.5 %collective-permute-start.3 = (bf16[512,1152]{1,0:T(8,128)(2,1)}, bf16[512,1152]{1,0:T(8,128)(2,1)S(1)}, u32[]{:S(2)}, u32[]{:S(2)}) collective-permute-start(bf16[512,1152]{1,0:T(8,128)(2,1)} %param.8), channel_id=1, source_target_pairs={{0,4},{4,0},{1,5},{5,1},{2,6},{6,2},{3,7},{7,3},{8,12},{12,8},{9,1... | collective-permute-start | bytes 3538952 | tf_op jit(solution)/shard_map/ppermute | solution.py:223
  152.2 2.5 copy-start.22
  154.8 1.3 copy-start.4
  156.1 36.3 %all-to-all-start.7 = ((bf16[8,96,1152]{2,1,0:T(8,128)(2,1)}), bf16[8,96,1152]{2,1,0:T(8,128)(2,1)S(1)}, u32[]{:S(2)}, u32[]{:S(2)}) async-start(bf16[8,96,1152]{2,1,0:T(8,128)(2,1)} %bitcast.122), calls=%async_computation.7 | async-start | bytes 3538944 | tf_op jit(solution)/shard_map/all_to_all | solution.py:231
  159.9 28.7 %collective-permute-start.4 = (bf16[512,1152]{1,0:T(8,128)(2,1)}, bf16[512,1152]{1,0:T(8,128)(2,1)}, u32[]{:S(2)}, u32[]{:S(2)}) collective-permute-start(bf16[512,1152]{1,0:T(8,128)(2,1)} %copy-done.22), channel_id=1, source_target_pairs={{0,2},{2,0},{1,3},{3,1},{4,6},{6,4},{5,7},{7,5},{8,10},{10,8},{9,1... | collective-permute-start | bytes 3538952 | tf_op jit(solution)/shard_map/ppermute | solution.py:224
  159.9 38.4 %collective-permute-start = (bf16[4,4,36,1152]{3,1,2,0:T(4,128)(2,1)}, bf16[4,4,36,1152]{3,1,2,0:T(4,128)(2,1)}, u32[]{:S(2)}, u32[]{:S(2)}) collective-permute-start(bf16[4,4,36,1152]{3,1,2,0:T(4,128)(2,1)} %copy-done.14), channel_id=1, source_target_pairs={{0,8},{8,0},{1,9},{9,1},{2,10},{10,2},{3,11},{11,3},{4,12},{12,4},... | collective-permute-start | bytes 3981320 | tf_op jit(solution)/shard_map/ppermute | solution.py:187
  192.4 1.3 copy-start.2
  193.7 34.5 %all-to-all-start.9 = ((bf16[8,96,1152]{2,1,0:T(8,128)(2,1)}), bf16[8,96,1152]{2,1,0:T(8,128)(2,1)}, u32[]{:S(2)}, u32[]{:S(2)}) async-start(bf16[8,96,1152]{2,1,0:T(8,128)(2,1)} %bitcast.22), calls=%async_computation.9 | async-start | bytes 3538944 | tf_op jit(solution)/shard_map/all_to_all | solution.py:231
  207.7 1.5 copy-start.5
  209.2 3.0 copy-start.10
  226.9 1.2 copy-start.8
  228.1 26.6 %all-to-all-start.6 = ((bf16[8,96,1152]{2,1,0:T(8,128)(2,1)}), bf16[8,96,1152]{2,1,0:T(8,128)(2,1)}, u32[]{:S(2)}, u32[]{:S(2)}) async-start(bf16[8,96,1152]{2,1,0:T(8,128)(2,1)} %bitcast.114), calls=%async_computation.6 | async-start | bytes 3538944 | tf_op jit(solution)/shard_map/all_to_all | solution.py:231
  232.6 3.0 copy-start.11
  251.3 1.3 copy-start.9
  254.7 26.6 %all-to-all-start.10 = ((bf16[8,96,1152]{2,1,0:T(8,128)(2,1)}), bf16[8,96,1152]{2,1,0:T(8,128)(2,1)}, u32[]{:S(2)}, u32[]{:S(2)}) async-start(bf16[8,96,1152]{2,1,0:T(8,128)(2,1)} %bitcast.115), calls=%async_computation.10 | async-start | bytes 3538944 | tf_op jit(solution)/shard_map/all_to_all | solution.py:231
  259.2 1.5 copy-start.3
  260.7 3.0 copy-start.12
  279.1 1.3 copy-start.7
  281.3 28.8 %all-to-all-start.8 = ((bf16[8,96,1152]{2,1,0:T(8,128)(2,1)}), bf16[8,96,1152]{2,1,0:T(8,128)(2,1)}, u32[]{:S(2)}, u32[]{:S(2)}) async-start(bf16[8,96,1152]{2,1,0:T(8,128)(2,1)} %bitcast.113), calls=%async_computation.8 | async-start | bytes 3538944 | tf_op jit(solution)/shard_map/all_to_all | solution.py:231
  289.4 30.2 %collective-permute-start.5 = (bf16[512,1152]{0,1:T(8,128)(2,1)}, bf16[512,1152]{0,1:T(8,128)(2,1)}, u32[]{:S(2)}, u32[]{:S(2)}) collective-permute-start(bf16[512,1152]{0,1:T(8,128)(2,1)} %convolution_convert_fusion.4), channel_id=1, source_target_pairs={{0,2},{2,0},{1,3},{3,1},{4,6},{6,4},{5,7},{7,5},{8,10},{10,8},{9,1... | collective-permute-start | bytes 3538952 | tf_op jit(solution)/shard_map/ppermute | solution.py:244
  289.8 1.5 copy-start.1
  291.3 3.0 copy-start.13
  309.0 1.2 copy-start.6
  310.2 26.8 %all-to-all-start.4 = ((bf16[8,96,1152]{2,1,0:T(8,128)(2,1)}), bf16[8,96,1152]{2,1,0:T(8,128)(2,1)}, u32[]{:S(2)}, u32[]{:S(2)}) async-start(bf16[8,96,1152]{2,1,0:T(8,128)(2,1)} %bitcast.112), calls=%async_computation.4 | async-start | bytes 3538944 | tf_op jit(solution)/shard_map/all_to_all | solution.py:231
  318.5 51.0 %collective-permute-start.2 = (bf16[512,1152]{0,1:T(8,128)(2,1)}, bf16[512,1152]{0,1:T(8,128)(2,1)}, u32[]{:S(2)}, u32[]{:S(2)}) collective-permute-start(bf16[512,1152]{0,1:T(8,128)(2,1)} %convolution_convert_fusion.5), channel_id=1, source_target_pairs={{0,2},{2,0},{1,3},{3,1},{4,6},{6,4},{5,7},{7,5},{8,10},{10,8},{9,1... | collective-permute-start | bytes 3538952 | tf_op jit(solution)/shard_map/ppermute | solution.py:246
  323.6 54.9 %collective-permute-start.6 = (bf16[512,1152]{0,1:T(8,128)(2,1)}, bf16[512,1152]{0,1:T(8,128)(2,1)}, u32[]{:S(2)}, u32[]{:S(2)}) collective-permute-start(bf16[512,1152]{0,1:T(8,128)(2,1)} %add_convert_fusion), channel_id=1, source_target_pairs={{0,4},{4,0},{1,5},{5,1},{2,6},{6,2},{3,7},{7,3},{8,12},{12,8},{9,1... | collective-permute-start | bytes 3538952 | tf_op jit(solution)/shard_map/ppermute | solution.py:245
  337.0 41.5 %copy-start.23 = (s32[512]{0:T(512)S(1)}, s32[512]{0:T(512)}, u32[]{:S(2)}) copy-start(s32[512]{0:T(512)} %param.14) | copy-start | bytes 6148
  398.5 5.0 %copy-start.21 = (bf16[512,1152]{1,0:T(8,128)(2,1)S(1)}, bf16[512,1152]{1,0:T(8,128)(2,1)}, u32[]{:S(2)}) copy-start(bf16[512,1152]{1,0:T(8,128)(2,1)} %param.8) | copy-start | bytes 3538948
  403.5 1.8 copy-start.16
  405.2 2.7 copy-start.15
  408.0 3.4 collective-permute-start.7
  444.7 15.3 %all-to-all-start.12 = ((bf16[4,36,1152]{2,1,0:T(8,128)(2,1)}), bf16[4,36,1152]{2,1,0:T(8,128)(2,1)S(1)}, u32[]{:S(2)}, u32[]{:S(2)}) async-start(bf16[4,36,1152]{2,1,0:T(8,128)(2,1)} %convert_element_type.102), calls=%async_computation.12 | async-start | bytes 737280 | tf_op jit(solution)/shard_map/all_to_all | solution.py:208
  449.7 10.3 %copy-start.17 = (f32[36,1152]{1,0:T(8,128)S(1)}, f32[36,1152]{1,0:T(8,128)}, u32[]{:S(2)}) copy-start(f32[36,1152]{1,0:T(8,128)} %param.9) | copy-start | bytes 497668
  449.7 10.3 %copy-start.19 = (f32[36,1152]{1,0:T(8,128)S(1)}, f32[36,1152]{1,0:T(8,128)}, u32[]{:S(2)}) copy-start(f32[36,1152]{1,0:T(8,128)} %param.10) | copy-start | bytes 497668
